TPU v7x, 256 devices: a whole 4x4x8 slice. The times are simulated.
256 devices in a mesh: gx: 8 (over z), gy: 16 (over y, x), gz: 2 (over core).
Axes of the slice: x: 4, y: 4, z: 8, core: 2. Of those that a mesh axis runs over, the one named last changes fastest.
Arguments:
- tensor: float32 [1024, 1024, 256], P('gx', 'gy', 'gz'), may hold values from -60 to 60
- factor_a: float32 [1024, 64], P(('gx', 'gy', 'gz')), may hold values from -6 to 6
- factor_b: float32 [1024, 64], P(('gy', 'gx', 'gz')), may hold values from -6 to 6
- factor_c: float32 [256, 64], P(('gz', 'gx', 'gy')), may hold values from -6 to 6
Outputs:
- slope_a: float32 [1024, 64], P(('gx', 'gy', 'gz'))
- slope_b: float32 [1024, 64], P(('gy', 'gx', 'gz'))
- slope_c: float32 [256, 64], P(('gz', 'gx', 'gy'))
All inputs are finite; a program needn't handle non-finite values.
Results may differ from a plain program's by a relative error of at most 0.0003.
Values sent between devices are 32-bit elements; how exact they have to be, the bound alone decides.
No kernel may reach another device: no remote copies, remote signals or barrier semaphores. Data moves between devices by JAX's collectives and lax.ppermute only.
A program may use at most 64 MiB of HBM per device.

v0:
```python
import jax
import jax.numpy as jnp
from jax import lax
from jax.sharding import PartitionSpec as P

STEPS = 2
step_size = 0.1


def gram_local(matrix):
    return jnp.dot(
        matrix.T, matrix, precision=lax.Precision.HIGHEST, preferred_element_type=jnp.float32
    )


def gather_blocks(own_a, own_b, own_c):
    block_a = lax.all_gather(own_a, ("gy", "gz"), axis=0, tiled=True)
    block_b = lax.all_gather(own_b, ("gx", "gz"), axis=0, tiled=True)
    block_c = lax.all_gather(own_c, ("gx", "gy"), axis=0, tiled=True)
    return (block_a, block_b, block_c)


def gram_sums(own_a, own_b, own_c):
    gram_a, gram_b, gram_c = lax.psum(
        (gram_local(own_a), gram_local(own_b), gram_local(own_c)), ("gx", "gy", "gz")
    )
    return (gram_a, gram_b, gram_c)


def partials(tensor, block_a, block_b, block_c):
    highest = lax.Precision.HIGHEST
    along_k = jnp.einsum("ijk,kr->jri", tensor, block_c, precision=highest)
    moment_a = jnp.einsum("jri,jr->ir", along_k, block_b, precision=highest)
    moment_b = jnp.einsum("jri,ir->jr", along_k, block_a, precision=highest)
    along_i = jnp.einsum("ijk,ir->rjk", tensor, block_a, precision=highest)
    moment_c = jnp.einsum("rjk,jr->kr", along_i, block_b, precision=highest)
    return (moment_a, moment_b, moment_c)


def slopes(first, second, third, moment_a, moment_b, moment_c, grams, counts):
    highest = lax.Precision.HIGHEST
    gram_a, gram_b, gram_c = grams
    count_i, count_j, count_k = counts
    slope_a = (jnp.dot(first, gram_b * gram_c, precision=highest) - moment_a) / (count_j * count_k)
    slope_b = (jnp.dot(second, gram_a * gram_c, precision=highest) - moment_b) / (count_i * count_k)
    slope_c = (jnp.dot(third, gram_a * gram_b, precision=highest) - moment_c) / (count_i * count_j)
    return (slope_a, slope_b, slope_c)


def shards(tensor, factor_a, factor_b, factor_c):
    counts = (
        float(tensor.shape[0] * lax.axis_size("gx")),
        float(tensor.shape[1] * lax.axis_size("gy")),
        float(tensor.shape[2] * lax.axis_size("gz")),
    )
    own_a, own_b, own_c = (factor_a, factor_b, factor_c)
    for round_index in range(STEPS):
        block_a, block_b, block_c = gather_blocks(own_a, own_b, own_c)
        grams = gram_sums(own_a, own_b, own_c)
        moment_a, moment_b, moment_c = partials(tensor, block_a, block_b, block_c)
        moment_a = lax.psum_scatter(moment_a, ("gy", "gz"), scatter_dimension=0, tiled=True)
        moment_b = lax.psum_scatter(moment_b, ("gx", "gz"), scatter_dimension=0, tiled=True)
        moment_c = lax.psum_scatter(moment_c, ("gx", "gy"), scatter_dimension=0, tiled=True)
        slope_a, slope_b, slope_c = slopes(
            own_a, own_b, own_c, moment_a, moment_b, moment_c, grams, counts
        )
        if round_index + 1 < STEPS:
            own_a = own_a - step_size * slope_a
            own_b = own_b - step_size * slope_b
            own_c = own_c - step_size * slope_c
    return (slope_a, slope_b, slope_c)


def solution(mesh):
    placed = (
        P("gx", "gy", "gz"),
        P(("gx", "gy", "gz"), None),
        P(("gy", "gx", "gz"), None),
        P(("gz", "gx", "gy"), None),
    )
    return jax.shard_map(
        shards,
        mesh=mesh,
        in_specs=placed,
        out_specs=(
            P(("gx", "gy", "gz"), None),
            P(("gy", "gx", "gz"), None),
            P(("gz", "gx", "gy"), None),
        ),
        check_vma=False,
    )
```

profile of v0, /device:TPU:1, one launch (start us, length us, event | category | flops | bytes accessed | tf_op | source)
XLA Modules:
  0.0 1523.7 jit_solution(15160832706329019883)
XLA Ops:
  7.2 0.0 all-reduce.11.cloned.1.call-start
  7.2 1.0 fusion.29
  8.2 21.6 %all-gather.1 = f32[16,4,64]{2,1,0:T(4,128)S(1)} all-gather(f32[1,4,64]{2,1,0:T(4,128)} %bitcast.117), channel_id=1, replica_groups=mesh['gx'=8,'gy'=16,'gz'=2] {'gx','gz'}, dimensions={0}, use_global_device_ids=true | all-gather | bytes 17408 | tf_op jit(solution)/shard_map/all_gather | solution.py:18
  29.8 284.8 %all-gather = f32[128,1,64]{2,1,0:T(1,128)S(1)} all-gather(f32[1,1,64]{2,1,0:T(1,128)} %bitcast.121), channel_id=1, replica_groups=mesh['gx'=8,'gy'=16,'gz'=2] {'gx','gy'}, dimensions={0}, use_global_device_ids=true | all-gather | bytes 33024 | tf_op jit(solution)/shard_map/all_gather | solution.py:19
  314.7 1.0 fusion.30
  315.7 77.7 %all-gather.2 = f32[32,4,64]{2,1,0:T(4,128)S(1)} all-gather(f32[1,4,64]{2,1,0:T(4,128)} %bitcast.118), channel_id=1, replica_groups=mesh['gx'=8,'gy'=16,'gz'=2] {'gy','gz'}, dimensions={0}, use_global_device_ids=true | all-gather | bytes 33792 | tf_op jit(solution)/shard_map/all_gather | solution.py:17
  393.4 0.1 copy.53
  393.5 0.1 copy.54
  393.5 9.2 fusion.9
  402.8 0.0 copy-start.2
  402.8 0.0 copy-start.5
  402.8 0.0 copy-start
  402.8 0.0 copy-start.4
  402.8 0.0 copy-start.1
  402.8 0.6 multiply_reduce_fusion.3
  403.4 42.5 %all-reduce.1 = f32[64,64]{1,0:T(8,128)S(1)} all-reduce(f32[64,64]{1,0:T(8,128)S(1)} %bitcast.113), channel_id=3, replica_groups=mesh['gx'=8,'gy'=16,'gz'=2] {'gx','gz'}, use_global_device_ids=true, to_apply=%region_4.0.clone | all-reduce | flops 4096 | bytes 32768
  446.0 0.0 copy-done.2
  446.0 0.1 broadcast_multiply_fusion.1
  446.1 0.0 copy-done.5
  446.1 0.6 dynamic-slice.2
  447.3 76.9 %all-reduce.7 = (f32[64,64]{1,0:T(8,128)S(1)}, f32[64,64]{1,0:T(8,128)S(1)}, f32[64,64]{1,0:T(8,128)S(1)}) all-reduce(f32[64,64]{1,0:T(8,128)S(1)} %fusion.29, f32[64,64]{1,0:T(8,128)S(1)} %broadcast_multiply_fusion.1, f32[64,64]{1,0:T(8,128)S(1)} %fusion.30), channel_id=1, replica_groups=mesh['gx'=8,'gy'=16,'gz'=2] {'gx','gy','gz'}, use_global_device_ids=true, to_apply=%region_0.0 | all-reduce | flops 12288 | bytes 98304 | tf_op jit(solution)/shard_map/psum | solution.py:24
  524.2 0.0 copy-done
  524.3 0.1 fusion.14
  524.4 17.3 %all-gather.3 = f32[16,4,64]{2,1,0:T(4,128)S(1)} all-gather(f32[1,4,64]{2,1,0:T(4,128)S(1)} %bitcast.115), channel_id=1, replica_groups=mesh['gx'=8,'gy'=16,'gz'=2] {'gx','gz'}, dimensions={0}, use_global_device_ids=true | all-gather | bytes 17408 | tf_op jit(solution)/shard_map/all_gather | solution.py:18
  541.8 0.1 copy.56
  541.8 0.0 copy-done.4
  541.8 0.6 dynamic-slice
  543.1 0.1 copy.21
  543.2 119.2 %all-reduce = f32[128,64]{1,0:T(8,128)S(1)} all-reduce(f32[128,64]{1,0:T(8,128)S(1)} %bitcast.111), channel_id=2, replica_groups=mesh['gx'=8,'gy'=16,'gz'=2] {'gy','gz'}, use_global_device_ids=true, to_apply=%region_2.0.clone | all-reduce | flops 8192 | bytes 65536
  662.3 0.0 copy-done.1
  662.3 0.1 fusion.17
  662.5 26.8 %all-gather.5 = f32[32,4,64]{2,1,0:T(4,128)S(1)} all-gather(f32[1,4,64]{2,1,0:T(4,128)S(1)} %bitcast.116), channel_id=1, replica_groups=mesh['gx'=8,'gy'=16,'gz'=2] {'gy','gz'}, dimensions={0}, use_global_device_ids=true | all-gather | bytes 33792 | tf_op jit(solution)/shard_map/all_gather | solution.py:17
  689.3 7.2 fusion
  696.5 2.4 multiply_reduce_fusion
  698.9 0.7 copy.52
  699.6 7.2 fusion.2
  706.8 0.0 copy-start.3
  706.8 2.4 multiply_reduce_fusion.2
  709.3 0.7 copy.33
  710.0 0.0 all-reduce.11.cloned.1.call-update
  710.0 0.2 fusion.31
  710.2 0.2 fusion.32
  710.5 0.0 copy-done.3
  710.5 0.6 dynamic-slice.4
  711.1 0.1 copy.55
  711.2 203.8 %all-reduce.11.cloned.1.call-done = (f32[128,64]{1,0:T(8,128)}, f32[128,64]{1,0:T(8,128)}) async-done(((f32[128,64]{1,0:T(8,128)}, f32[128,64]{1,0:T(8,128)}), (f32[128,64]{1,0:T(8,128)}, f32[128,64]{1,0:T(8,128)})) %all-reduce.11.cloned.1.call-update) | async-done | bytes 65552
  914.9 1.5 fusion.19
  916.4 0.1 broadcast_multiply_fusion
  916.5 285.2 %all-gather.4 = f32[128,1,64]{2,1,0:T(1,128)S(1)} all-gather(f32[1,1,64]{2,1,0:T(1,128)S(1)} %bitcast.120), channel_id=1, replica_groups=mesh['gx'=8,'gy'=16,'gz'=2] {'gx','gy'}, dimensions={0}, use_global_device_ids=true | all-gather | bytes 33024 | tf_op jit(solution)/shard_map/all_gather | solution.py:19
  1201.6 9.3 fusion.8
  1210.9 0.6 multiply_reduce_fusion.1
  1211.5 103.3 %all-reduce.4 = f32[64,64]{1,0:T(8,128)S(1)} all-reduce(f32[64,64]{1,0:T(8,128)S(1)} %bitcast.114), channel_id=6, replica_groups=mesh['gx'=8,'gy'=16,'gz'=2] {'gx','gz'}, use_global_device_ids=true, to_apply=%region_10.0.clone | all-reduce | flops 4096 | bytes 32768
  1314.8 0.1 copy.40
  1314.9 121.7 %all-reduce.3 = f32[128,64]{1,0:T(8,128)S(1)} all-reduce(f32[128,64]{1,0:T(8,128)S(1)} %bitcast.112), channel_id=5, replica_groups=mesh['gx'=8,'gy'=16,'gz'=2] {'gy','gz'}, use_global_device_ids=true, to_apply=%region_8.0.clone | all-reduce | flops 8192 | bytes 65536
  1436.6 76.7 %all-reduce.6 = (f32[64,64]{1,0:T(8,128)S(1)}, f32[64,64]{1,0:T(8,128)S(1)}, f32[64,64]{1,0:T(8,128)S(1)}) all-reduce(f32[64,64]{1,0:T(8,128)S(1)} %fusion.31, f32[64,64]{1,0:T(8,128)S(1)} %broadcast_multiply_fusion, f32[64,64]{1,0:T(8,128)S(1)} %fusion.32), channel_id=1, replica_groups=mesh['gx'=8,'gy'=16,'gz'=2] {'gx','gy','gz'}, use_global_device_ids=true, to_apply=%region_5.0 | all-reduce | flops 12288 | bytes 98304 | tf_op jit(solution)/shard_map/psum | solution.py:24
  1513.4 2.0 fusion.20
  1515.4 0.7 fusion.10
  1516.1 0.7 fusion.11
Async XLA Ops:
  7.2 907.8 %all-reduce.11.cloned.1.call-start = ((), (), s32[]{:S(2)}) async-start(), calls=%async_computation | async-start | bytes 262144
  402.8 43.2 %copy-start.2 = (f32[1,64]{1,0:T(1,128)S(1)}, f32[1,64]{1,0:T(1,128)}, u32[]{:S(2)}) copy-start(f32[1,64]{1,0:T(1,128)} %param.7) | copy-start | bytes 772
  402.8 43.3 %copy-start.5 = (u32[256]{0:T(256)S(1)}, u32[256]{0:T(256)}, u32[]{:S(2)}) copy-start(u32[256]{0:T(256)} %constant.32) | copy-start | bytes 3076
  402.8 121.5 %copy-start = (f32[4,64]{1,0:T(4,128)S(1)}, f32[4,64]{1,0:T(4,128)}, u32[]{:S(2)}) copy-start(f32[4,64]{1,0:T(4,128)} %param.6) | copy-start | bytes 3076
  402.8 139.0 %copy-start.4 = (u32[256]{0:T(256)S(1)}, u32[256]{0:T(256)}, u32[]{:S(2)}) copy-start(u32[256]{0:T(256)} %constant.28) | copy-start | bytes 3076
  402.8 259.5 %copy-start.1 = (f32[4,64]{1,0:T(4,128)S(1)}, f32[4,64]{1,0:T(4,128)}, u32[]{:S(2)}) copy-start(f32[4,64]{1,0:T(4,128)} %param.5) | copy-start | bytes 3076
  706.8 3.7 copy-start.3
Sparse Core Ops, SparseCore 0:
  710.1 204.7 all-reduce.10
where the time goes:
time: 1520 us
  blocking collectives  1250 us (82%)
  waiting for transfers between devices  204 us (13%)
  matrix products  40.5 us (3%)
  between operations  15.5 us (1%)
    all_gather x2, blocking collectives, gather_blocks(): block_c = lax.all_gather(own_c, ('gx', 'gy'), axis=0, tiled=True)  570 us
    unnamed x4, blocking collectives  387 us
    unnamed x2, waiting for transfers between devices  204 us
    psum x2, blocking collectives, gram_sums(): lax.psum((gram_local(own_a), gram_local(own_b), gram_local(own_c)), ('gx'...  154 us
    all_gather x2, blocking collectives, gather_blocks(): block_a = lax.all_gather(own_a, ('gy', 'gz'), axis=0, tiled=True)  105 us
    all_gather x2, blocking collectives, gather_blocks(): block_b = lax.all_gather(own_b, ('gx', 'gz'), axis=0, tiled=True)  39 us
  transfers between devices with their start and end apart: 1, of which 1 were waited for; matrix products, arithmetic and copies ran while one was open for 0% of the time, Pallas kernels for 0%

commit v1 on v0

--- a/solution.py
+++ b/solution.py
@@ -22,7 +22,7 @@
 
 def gram_sums(own_a, own_b, own_c):
     gram_a, gram_b, gram_c = lax.psum(
-        (gram_local(own_a), gram_local(own_b), gram_local(own_c)), ("gx", "gy", "gz")
+        lax.psum((gram_local(own_a), gram_local(own_b), gram_local(own_c)), "gx"), ("gy", "gz")
     )
     return (gram_a, gram_b, gram_c)
 

time: 1520 us -> 1270 us (0.84)
  blocking collectives: 1250 us -> 914 us
  waiting for transfers between devices: 204 us -> 287 us
    unnamed x4 -> x2, blocking collectives: 387 us -> 155 us
    psum x2, blocking collectives: 154 us -> 43.9 us  [gram_sums(): lax.psum((gram_local(own_a), gram_local(own_b), gram_local(own_c)), 'gx')]
    psum x0 -> x2, waiting for transfers between devices: none -> 83.3 us  [gram_sums(): lax.psum(lax.psum((gram_local(own_a), gram_local(own_b), gram_local(own_c...]
    unnamed x2 -> x4, waiting for transfers between devices: 204 us -> 204 us
  transfers between devices with their start and end apart: 1 -> 3, of which waited for: 1 -> 3; matrix products, arithmetic and copies ran while one was open for 0% -> 1% of each run, Pallas kernels for 0% -> 0%
where the time goes in v1:
time: 1270 us
  blocking collectives  914 us (72%)
  waiting for transfers between devices  287 us (23%)
  matrix products  43.7 us (3%)
  between operations  15.2 us (1%)
    all_gather x2, blocking collectives, gather_blocks(): block_c = lax.all_gather(own_c, ('gx', 'gy'), axis=0, tiled=True)  570 us
    unnamed x4, waiting for transfers between devices  204 us
    unnamed x2, blocking collectives  155 us
    all_gather x2, blocking collectives, gather_blocks(): block_a = lax.all_gather(own_a, ('gy', 'gz'), axis=0, tiled=True)  107 us
    psum x2, waiting for transfers between devices, gram_sums(): lax.psum(lax.psum((gram_local(own_a), gram_local(own_b), gram_local(own_c...  83.3 us
    psum x2, blocking collectives, gram_sums(): lax.psum((gram_local(own_a), gram_local(own_b), gram_local(own_c)), 'gx')  43.9 us
    all_gather x2, blocking collectives, gather_blocks(): block_b = lax.all_gather(own_b, ('gx', 'gz'), axis=0, tiled=True)  39 us
  transfers between devices with their start and end apart: 3, of which 3 were waited for; matrix products, arithmetic and copies ran while one was open for 1% of the time, Pallas kernels for 0%

profile of v1, /device:TPU:1, one launch (start us, length us, event | category | flops | bytes accessed | tf_op | source)
XLA Modules:
  0.0 1272.3 jit_solution(5839829745743680472)
XLA Ops:
  7.2 0.0 all-reduce.19.cloned.1.call-start
  7.2 0.8 broadcast_multiply_fusion.1
  8.0 1.0 fusion.29
  9.0 21.6 %all-gather.1 = f32[16,4,64]{2,1,0:T(4,128)S(1)} all-gather(f32[1,4,64]{2,1,0:T(4,128)} %bitcast.117), channel_id=1, replica_groups=mesh['gx'=8,'gy'=16,'gz'=2] {'gx','gz'}, dimensions={0}, use_global_device_ids=true | all-gather | bytes 17408 | tf_op jit(solution)/shard_map/all_gather | solution.py:18
  30.6 1.0 fusion.30
  31.6 284.8 %all-gather = f32[128,1,64]{2,1,0:T(1,128)S(1)} all-gather(f32[1,1,64]{2,1,0:T(1,128)} %bitcast.122), channel_id=1, replica_groups=mesh['gx'=8,'gy'=16,'gz'=2] {'gx','gy'}, dimensions={0}, use_global_device_ids=true | all-gather | bytes 33024 | tf_op jit(solution)/shard_map/all_gather | solution.py:19
  316.5 9.2 fusion.9
  325.7 0.7 copy.21
  326.4 21.8 %all-reduce.10 = (f32[64,64]{1,0:T(8,128)}, f32[64,64]{1,0:T(8,128)}, f32[64,64]{1,0:T(8,128)}) all-reduce(f32[64,64]{1,0:T(8,128)S(1)} %fusion.29, f32[64,64]{1,0:T(8,128)S(1)} %broadcast_multiply_fusion.1, f32[64,64]{1,0:T(8,128)S(1)} %fusion.30), channel_id=1, replica_groups=mesh['gx'=8,'gy'=16,'gz'=2] {'gx'}, use_global_device_ids=true, to_apply=%region_0.0 | all-reduce | flops 12288 | bytes 98304 | tf_op jit(solution)/shard_map/psum | solution.py:25
  348.3 0.0 all-reduce.19.cloned.1.call-update
  348.3 0.0 all-reduce.15.cloned.1.call-start
  348.3 0.1 copy.54
  348.4 0.0 copy-done.3
  348.4 83.8 %all-gather.2 = f32[32,4,64]{2,1,0:T(4,128)S(1)} all-gather(f32[1,4,64]{2,1,0:T(4,128)S(1)} %bitcast.118), channel_id=1, replica_groups=mesh['gx'=8,'gy'=16,'gz'=2] {'gy','gz'}, dimensions={0}, use_global_device_ids=true | all-gather | bytes 33792 | tf_op jit(solution)/shard_map/all_gather | solution.py:17
  432.2 0.1 copy.53
  432.2 7.2 fusion.2
  439.5 0.0 copy-start.7
  439.5 0.0 copy-start.6
  439.5 0.0 copy-start.5
  439.5 0.0 copy-start.2
  439.5 2.4 multiply_reduce_fusion.2
  441.9 0.6 multiply_reduce_fusion.3
  442.6 0.0 copy-done.7
  442.6 0.6 dynamic-slice.4
  443.1 0.0 copy-done.6
  443.2 0.6 dynamic-slice.2
  443.7 0.0 copy-done.5
  443.7 0.6 dynamic-slice
  445.6 0.7 copy.33
  446.3 44.4 %all-reduce.1 = f32[64,64]{1,0:T(8,128)S(1)} all-reduce(f32[64,64]{1,0:T(8,128)S(1)} %bitcast.113), channel_id=3, replica_groups=mesh['gx'=8,'gy'=16,'gz'=2] {'gx','gz'}, use_global_device_ids=true, to_apply=%region_7.0.clone | all-reduce | flops 4096 | bytes 32768
  490.8 23.5 %all-reduce.19.cloned.1.call-done = (f32[64,64]{1,0:T(8,128)}, f32[64,64]{1,0:T(8,128)}, f32[128,64]{1,0:T(8,128)}, f32[64,64]{1,0:T(8,128)}) async-done(((f32[64,64]{1,0:T(8,128)}, f32[64,64]{1,0:T(8,128)}, f32[128,64]{1,0:T(8,128)}, f32[64,64]{1,0:T(8,128)}), (f32[64,64]{1,0:T(8,128)}, f32[64,64]{1,0:T(8,128)}, f32[128,64]{1,0:T(8,128)}, f32[64,64]{1,0:T(8,128)})) %all-reduce.19.cloned.1.call-update) | async-done | bytes 81936 | tf_op jit(solution)/shard_map/psum | solution.py:24
  514.2 0.0 copy-done.2
  514.2 0.9 fusion.14
  515.1 17.4 %all-gather.3 = f32[16,4,64]{2,1,0:T(4,128)S(1)} all-gather(f32[1,4,64]{2,1,0:T(4,128)S(1)} %bitcast.116), channel_id=1, replica_groups=mesh['gx'=8,'gy'=16,'gz'=2] {'gx','gz'}, dimensions={0}, use_global_device_ids=true | all-gather | bytes 17408 | tf_op jit(solution)/shard_map/all_gather | solution.py:18
  532.5 0.1 copy.56
  532.6 0.9 fusion.17
  533.5 0.2 fusion.32
  533.8 23.0 %all-gather.5 = f32[32,4,64]{2,1,0:T(4,128)S(1)} all-gather(f32[1,4,64]{2,1,0:T(4,128)S(1)} %bitcast.115), channel_id=1, replica_groups=mesh['gx'=8,'gy'=16,'gz'=2] {'gy','gz'}, dimensions={0}, use_global_device_ids=true | all-gather | bytes 33792 | tf_op jit(solution)/shard_map/all_gather | solution.py:17
  556.8 7.2 fusion
  564.0 0.0 copy-start
  564.0 0.0 copy-start.1
  564.0 0.0 copy-start.4
  564.0 2.4 multiply_reduce_fusion
  566.5 0.7 copy.52
  567.2 0.0 all-reduce.15.cloned.1.call-update
  567.2 0.0 all-reduce.17.cloned.1.call-start
  567.2 0.2 fusion.31
  567.5 0.1 copy.55
  567.6 204.0 %all-reduce.15.cloned.1.call-done = (f32[128,64]{1,0:T(8,128)}, f32[128,64]{1,0:T(8,128)}) async-done(((f32[128,64]{1,0:T(8,128)}, f32[128,64]{1,0:T(8,128)}), (f32[128,64]{1,0:T(8,128)}, f32[128,64]{1,0:T(8,128)})) %all-reduce.15.cloned.1.call-update) | async-done | bytes 65552
  771.5 0.0 copy-done
  771.5 0.0 copy-done.1
  771.5 1.5 fusion.19
  773.0 0.1 broadcast_multiply_fusion
  773.1 285.0 %all-gather.4 = f32[128,1,64]{2,1,0:T(1,128)S(1)} all-gather(f32[1,1,64]{2,1,0:T(1,128)S(1)} %bitcast.120), channel_id=1, replica_groups=mesh['gx'=8,'gy'=16,'gz'=2] {'gx','gy'}, dimensions={0}, use_global_device_ids=true | all-gather | bytes 33024 | tf_op jit(solution)/shard_map/all_gather | solution.py:19
  1058.0 9.2 fusion.8
  1067.3 0.7 copy.40
  1068.0 22.1 %all-reduce.9 = (f32[64,64]{1,0:T(8,128)}, f32[64,64]{1,0:T(8,128)}, f32[64,64]{1,0:T(8,128)}) all-reduce(f32[64,64]{1,0:T(8,128)S(1)} %fusion.31, f32[64,64]{1,0:T(8,128)S(1)} %broadcast_multiply_fusion, f32[64,64]{1,0:T(8,128)S(1)} %fusion.32), channel_id=1, replica_groups=mesh['gx'=8,'gy'=16,'gz'=2] {'gx'}, use_global_device_ids=true, to_apply=%region_8.0 | all-reduce | flops 12288 | bytes 98304 | tf_op jit(solution)/shard_map/psum | solution.py:25
  1090.1 0.0 all-reduce.17.cloned.1.call-update
  1090.1 0.6 multiply_reduce_fusion.1
  1090.8 110.1 %all-reduce.4 = f32[64,64]{1,0:T(8,128)S(1)} all-reduce(f32[64,64]{1,0:T(8,128)S(1)} %bitcast.114), channel_id=6, replica_groups=mesh['gx'=8,'gy'=16,'gz'=2] {'gx','gz'}, use_global_device_ids=true, to_apply=%region_16.0.clone | all-reduce | flops 4096 | bytes 32768
  1200.9 59.8 %all-reduce.17.cloned.1.call-done = (f32[64,64]{1,0:T(8,128)}, f32[64,64]{1,0:T(8,128)}, f32[128,64]{1,0:T(8,128)}, f32[64,64]{1,0:T(8,128)}) async-done(((f32[64,64]{1,0:T(8,128)}, f32[64,64]{1,0:T(8,128)}, f32[128,64]{1,0:T(8,128)}, f32[64,64]{1,0:T(8,128)}), (f32[64,64]{1,0:T(8,128)}, f32[64,64]{1,0:T(8,128)}, f32[128,64]{1,0:T(8,128)}, f32[64,64]{1,0:T(8,128)})) %all-reduce.17.cloned.1.call-update) | async-done | bytes 81936 | tf_op jit(solution)/shard_map/psum | solution.py:24
  1260.7 1.5 fusion.10
  1262.2 2.1 fusion.20
  1264.3 1.5 fusion.11
  (2 shorter events, 0.0 us)
Async XLA Ops:
  7.2 507.0 %all-reduce.19.cloned.1.call-start = ((), (), s32[]{:S(2)}) async-start(), calls=%async_computation.2 | async-start | bytes 327680 | tf_op jit(solution)/shard_map/psum | solution.py:24
  316.5 31.9 %copy-start.3 = (f32[4,64]{1,0:T(4,128)S(1)}, f32[4,64]{1,0:T(4,128)}, u32[]{:S(2)}) copy-start(f32[4,64]{1,0:T(4,128)} %param.5) | copy-start | bytes 3076
  348.3 423.3 %all-reduce.15.cloned.1.call-start = ((), (), s32[]{:S(2)}) async-start(), calls=%async_computation | async-start | bytes 262144
  439.5 3.1 copy-start.7
  439.5 3.7 copy-start.6
  439.5 4.3 copy-start.5
  439.5 74.7 %copy-start.2 = (f32[4,64]{1,0:T(4,128)S(1)}, f32[4,64]{1,0:T(4,128)}, u32[]{:S(2)}) copy-start(f32[4,64]{1,0:T(4,128)} %param.6) | copy-start | bytes 3076
  564.0 207.5 %copy-start = (f32[64,64]{1,0:T(8,128)S(1)}, f32[64,64]{1,0:T(8,128)}, u32[]{:S(2)}) copy-start(f32[64,64]{1,0:T(8,128)} %get-tuple-element.9) | copy-start | bytes 49156
  564.0 207.5 %copy-start.1 = (f32[64,64]{1,0:T(8,128)S(1)}, f32[64,64]{1,0:T(8,128)}, u32[]{:S(2)}) copy-start(f32[64,64]{1,0:T(8,128)} %get-tuple-element.12) | copy-start | bytes 49156
  564.0 207.5 %copy-start.4 = (f32[1,64]{1,0:T(1,128)S(1)}, f32[1,64]{1,0:T(1,128)}, u32[]{:S(2)}) copy-start(f32[1,64]{1,0:T(1,128)} %param.7) | copy-start | bytes 772
  567.2 693.5 %all-reduce.17.cloned.1.call-start = ((), (), s32[]{:S(2)}) async-start(), calls=%async_computation.1 | async-start | bytes 327680 | tf_op jit(solution)/shard_map/psum | solution.py:24
Sparse Core Ops, SparseCore 0:
  348.4 165.7 all-reduce.18
  567.3 204.1 all-reduce.14
  1090.3 170.3 all-reduce.16
